TPU v7x, 128 devices: a whole 4x4x4 slice. The times are simulated.
128 devices in a mesh: group: 8 (over z, core), pair: 16 (over y, x).
Axes of the slice: x: 4, y: 4, z: 4, core: 2. Of those that a mesh axis runs over, the one named last changes fastest.
Arguments:
- query_embed: bfloat16 [8, 16, 1024], P('group'), may hold values from -6 to 6
- teacher_scores: float32 [8, 16, 16, 32], P('group', 'pair'), may hold values from -9 to 9
- pair_owner: int32 [8, 16, 16, 32, 1], P('group', 'pair'), may hold values from 0 to 127; in each aligned block of 512 rows (0 to 511, 512 to 1023, ..., all dimensions but the last counted through in order) at most 8 rows name the same one
- pair_row: int32 [8, 16, 16, 32], P('group', 'pair'), may hold values from 0 to 2047
- passage_hidden: bfloat16 [262144, 1024], P(('group', 'pair')), may hold values from -24 to 24
- projection: bfloat16 [1024, 1024], replicated, may hold values from -0.1875 to 0.1875
Outputs:
- query_loss: float32 [8, 16], P('group', 'pair')
- query_grad: float32 [8, 16, 1024], P('group', 'pair')
- hidden_grad: bfloat16 [262144, 1024], P(('group', 'pair'))
- projection_grad: float32 [1024, 1024], P(('group', 'pair'))
Inputs may be any that keep to these rules, and one draw needn't show every extreme that they name: `pair_owner`: owners are numbered with group as the slower index. Among the 512 candidates held by one device, at most 8 name the same owner, and every draw has a device and an owner with exactly 8. `pair_row`: A passage may be named by several candidates.
All inputs are finite; a program needn't handle non-finite values.
Results may differ from a plain program's by a relative error of at most 0.022.
Values may be sent and summed in bfloat16 or wider, within the bound.
A program may use at most 128 MiB of HBM per device.

v0:
```python
import math
import jax
import jax.numpy as jnp
from jax import lax
from jax.sharding import PartitionSpec as P

loss_scale = 1024.0


def soft_steps(values_all, values_own):
    return jax.nn.sigmoid((values_all[:, None, :] - values_own[:, :, None]) * 2.0)


def score_slope(soft_step, grad_all, grad_own):
    slopes = soft_step * (1.0 - soft_step)
    return 2.0 * (jnp.sum(slopes * grad_all[:, None, :], -1) - grad_own * jnp.sum(slopes, -1))


def shards(query_embed, teacher_scores, pair_owner, pair_row, passage_hidden, projection):
    model_width = query_embed.shape[2]
    query_rows = query_embed.shape[1]
    cand_dev = teacher_scores.shape[3]
    pass_rows = passage_hidden.shape[0]
    pair_size = lax.axis_size("pair")
    group_size = lax.axis_size("group")
    devices = pair_size * group_size
    cand_all = cand_dev * pair_size
    pair_count = query_rows * cand_dev
    capacity = max(2, 2 * pair_count // devices)
    query_dev = query_rows // pair_size
    inv_root = 1.0 / math.sqrt(model_width)
    spearman_den = float(cand_all * (cand_all * cand_all - 1))
    embedded = jnp.dot(passage_hidden, projection, preferred_element_type=jnp.float32).astype(
        jnp.bfloat16
    )
    owner_dev = pair_owner.reshape(pair_count)
    row_index = pair_row.reshape(pair_count)
    owner_marks = (owner_dev[:, None] == jnp.arange(devices, dtype=jnp.int32)[None, :]).astype(
        jnp.int32
    )
    slot_index = jnp.sum(jnp.cumsum(owner_marks, axis=0) * owner_marks, axis=1) - 1
    requests = jnp.zeros((devices, capacity), jnp.int32).at[owner_dev, slot_index].set(row_index)
    queries = query_embed[0]
    asked_rows = lax.all_to_all(
        requests, ("group", "pair"), split_axis=0, concat_axis=0, tiled=True
    )
    vectors = jnp.take(embedded, asked_rows, axis=0)
    replies = lax.all_to_all(vectors, ("group", "pair"), split_axis=0, concat_axis=0, tiled=True)
    pair_vectors = replies[owner_dev, slot_index].reshape(query_rows, cand_dev, model_width)
    scores = (
        jnp.einsum("qd,qcd->qc", queries, pair_vectors, preferred_element_type=jnp.float32)
        * inv_root
    )
    teacher_own = teacher_scores.reshape(query_rows, cand_dev)
    scores_all, teacher_all = (
        lax.all_gather(scores, "pair", axis=1, tiled=True),
        lax.all_gather(teacher_own, "pair", axis=1, tiled=True),
    )
    soft_step = soft_steps(scores_all, scores)
    rank_student = 0.5 + jnp.sum(soft_step, -1)
    rank_teacher = 0.5 + jnp.sum(soft_steps(teacher_all, teacher_own), -1)
    rank_gap = rank_student - rank_teacher
    loss_part = 6.0 * jnp.sum(rank_gap * rank_gap, axis=1) / spearman_den
    rank_grad = loss_scale * 12.0 * rank_gap / spearman_den
    grad_all = lax.all_gather(rank_grad, "pair", axis=1, tiled=True)
    score_grad = score_slope(soft_step, grad_all, rank_grad)
    query_part = (
        jnp.sum(score_grad[:, :, None] * pair_vectors.astype(jnp.float32), axis=1) * inv_root
    )
    pair_grad = (
        score_grad[:, :, None] * queries.astype(jnp.float32)[:, None, :] * inv_root
    ).astype(jnp.bfloat16)
    query_sum, loss_own = (
        lax.psum_scatter(
            query_part.astype(jnp.bfloat16), "pair", scatter_dimension=0, tiled=True
        ).astype(jnp.float32),
        lax.psum_scatter(
            loss_part.astype(jnp.bfloat16), "pair", scatter_dimension=0, tiled=True
        ).astype(jnp.float32),
    )
    outgoing = (
        jnp.zeros((devices, capacity, model_width), jnp.bfloat16)
        .at[owner_dev, slot_index]
        .set(pair_grad.reshape(pair_count, model_width))
    )
    arrived = lax.all_to_all(outgoing, ("group", "pair"), split_axis=0, concat_axis=0, tiled=True)
    embed_grad = (
        jnp.zeros((pass_rows, model_width), jnp.float32)
        .at[asked_rows.reshape(-1)]
        .add(arrived.reshape(-1, model_width).astype(jnp.float32))
    )
    grad_rounded = embed_grad.astype(jnp.bfloat16)
    hidden_grad = jnp.einsum(
        "pe,de->pd", grad_rounded, projection, preferred_element_type=jnp.float32
    ).astype(jnp.bfloat16)
    projection_grad = lax.psum_scatter(
        jnp.einsum("pr,pe->re", passage_hidden, grad_rounded, preferred_element_type=jnp.float32),
        ("group", "pair"),
        scatter_dimension=0,
        tiled=True,
    )
    return (
        loss_own.reshape(1, query_dev),
        query_sum.reshape(1, query_dev, model_width),
        hidden_grad,
        projection_grad,
    )


def solution(mesh):
    placed = (
        P("group", None, None),
        P("group", "pair", None, None),
        P("group", "pair", None, None, None),
        P("group", "pair", None, None),
        P(("group", "pair"), None),
        P(),
    )
    return jax.shard_map(
        shards,
        mesh=mesh,
        in_specs=placed,
        out_specs=(
            P("group", "pair"),
            P("group", "pair", None),
            P(("group", "pair"), None),
            P(("group", "pair"), None),
        ),
        check_vma=False,
    )
```

profile of v0, /device:TPU:0, one launch (start us, length us, event | category | flops | bytes accessed | tf_op | source)
XLA Modules:
  0.0 964.4 jit_solution(8039499689911197415)
XLA Ops:
  10.2 1.4 reduce.10
  12.3 22.0 %scatter_fusion = s32[128,8]{0,1:T(8,128)S(1)} fusion(s32[128,8]{0,1:T(8,128)S(1)} %broadcast_in_dim.18, s32[512]{0:T(512)S(1)} %bitcast.82, s32[512]{0:T(512)S(1)} %reshape.243), kind=kCustom, calls=%fused_computation.2 | custom fusion | bytes 10240 | tf_op jit(solution)/shard_map/scatter | solution.py:42
  35.0 11.1 %all-to-all-start = ((s32[128,1,8]{2,1,0:T(1,128)}), s32[128,1,8]{2,1,0:T(1,128)S(1)}, u32[]{:S(2)}, u32[]{:S(2)}) async-start(s32[128,1,8]{2,1,0:T(1,128)} %copy.31), calls=%async_computation | async-start | bytes 131072 | tf_op jit(solution)/shard_map/all_to_all | solution.py:44
  46.2 8.3 convolution_convert_fusion.1
  56.0 8.8 gather_fusion
  64.7 3.2 bitcast_select_fusion
  67.9 9.1 all-to-all-start.1
  77.1 41.4 %all-gather = f32[1,1,16,512]{2,1,0,3:T(1,128)S(1)} all-gather(f32[1,1,16,32]{2,1,0,3:T(1,128)S(1)} %copy.35), channel_id=2, replica_groups=mesh['group'=8,'pair'=16] {'pair'}, dimensions={3}, use_global_device_ids=true | all-gather | bytes 34816 | tf_op jit(solution)/shard_map/all_gather | solution.py:57
  119.1 7.7 gather_fusion.1
  127.2 22.0 %all-gather.1 = f32[16,32,16]{1,2,0:T(8,128)S(1)} all-gather(f32[1,32,16]{1,2,0:T(8,128)S(1)} %get-tuple-element.28), channel_id=1, replica_groups=mesh['group'=8,'pair'=16] {'pair'}, dimensions={0}, use_global_device_ids=true | all-gather | bytes 34816 | tf_op jit(solution)/shard_map/all_gather | solution.py:56
  149.9 22.6 %all-gather.2 = f32[16,32,16]{1,2,0:T(8,128)S(1)} all-gather(f32[1,32,16]{1,2,0:T(8,128)S(1)} %multiply_bitcast_fusion), channel_id=1, replica_groups=mesh['group'=8,'pair'=16] {'pair'}, dimensions={0}, use_global_device_ids=true | all-gather | bytes 34816 | tf_op jit(solution)/shard_map/all_gather | solution.py:65
  173.4 1.2 fusion.5
  174.7 1.6 broadcast_in_dim.23
  176.2 73.0 %scatter_fusion.1 = bf16[128,8,1024]{2,1,0:T(8,128)(2,1)} fusion(bf16[128,8,1024]{2,1,0:T(8,128)(2,1)} %broadcast_in_dim.23, s32[512]{0:T(512)S(1)} %bitcast.83, bf16[512,1024]{1,0:T(8,128)(2,1)} %fusion.5), kind=kCustom, calls=%fused_computation.3 | custom fusion | bytes 3149824 | tf_op jit(solution)/shard_map/scatter | solution.py:84
  249.2 8.3 all-to-all-start.2
  258.5 28.3 %all-to-all-done.2 = bf16[128,8,1024]{2,1,0:T(8,128)(2,1)} async-done(((bf16[128,8,1024]{2,1,0:T(8,128)(2,1)}), bf16[128,8,1024]{2,1,0:T(8,128)(2,1)}, u32[]{:S(2)}, u32[]{:S(2)}) %all-to-all-start.2) | async-done | bytes 2097184 | tf_op jit(solution)/shard_map/all_to_all | solution.py:86
  286.8 13.4 %scatter_custom_fusion.2 = f32[2048,1024]{1,0:T(8,128)} fusion(s32[1024]{0:T(1024)S(1)} %bitcast.101, f32[]{:T(128)} %constant.26.clone.1, bf16[128,8,1024]{2,1,0:T(8,128)(2,1)} %all-to-all-done.2), kind=kCustom, calls=%fused_computation.5 | custom fusion | flops 2097152 | bytes 10485764 | tf_op jit(solution)/shard_map/scatter-add | solution.py:90
  300.2 11.2 %convolution_bitcast_fusion = f32[1024,1024]{0,1:T(8,128)} fusion(bf16[2048,1024]{1,0:T(8,128)(2,1)} %param.10, f32[2048,1024]{1,0:T(8,128)} %scatter_custom_fusion.2), kind=kOutput, calls=%fused_computation.10 | convolution fusion | flops 4297064448 | bytes 16777216 | tf_op jit(solution)/shard_map/pr,pe->re/dot_general | solution.py:97
  311.3 5.3 copy.41
  317.9 72.1 %all-reduce.2 = (bf16[16]{0:T(256)(128)(2,1)S(1)}, bf16[16,1024]{1,0:T(8,128)(2,1)S(1)}) all-reduce(bf16[16]{0:T(256)(128)(2,1)S(1)} %multiply_convert_fusion.1, bf16[16,1024]{1,0:T(8,128)(2,1)S(1)} %multiply_convert_fusion), channel_id=3, replica_groups=mesh['group'=8,'pair'=16] {'pair'}, use_global_device_ids=true, to_apply=%region_7.8.clone | all-reduce | flops 16400 | bytes 65600
  390.0 1.2 dynamic-slice.1
  391.9 1.2 bitcast_convert_fusion.1
  393.2 9.5 convolution_convert_fusion
  402.6 553.7 %reduce-scatter.4.cloned.1.call-done = f32[8,1024]{1,0:T(8,128)} async-done(((f32[1024,1024]{1,0:T(8,128)}), f32[8,1024]{1,0:T(8,128)}) %reduce-scatter.4.cloned.1.call-update) | async-done | bytes 32784
  (58 shorter events, 10.7 us)
Async XLA Ops:
  7.2 39.0 %copy-start = (bf16[1024,1024]{1,0:T(8,128)(2,1)S(1)}, bf16[1024,1024]{1,0:T(8,128)(2,1)}, u32[]{:S(2)}) copy-start(bf16[1024,1024]{1,0:T(8,128)(2,1)} %param.11) | copy-start | bytes 6291460
  35.0 20.6 %all-to-all-start = ((s32[128,1,8]{2,1,0:T(1,128)}), s32[128,1,8]{2,1,0:T(1,128)S(1)}, u32[]{:S(2)}, u32[]{:S(2)}) async-start(s32[128,1,8]{2,1,0:T(1,128)} %copy.31), calls=%async_computation | async-start | bytes 131072 | tf_op jit(solution)/shard_map/all_to_all | solution.py:44
  64.7 12.3 %copy-start.2 = (f32[1,1,16,32]{3,2,1,0:T(8,128)S(1)}, f32[1,1,16,32]{3,2,1,0:T(8,128)}, u32[]{:S(2)}) copy-start(f32[1,1,16,32]{3,2,1,0:T(8,128)} %param.7) | copy-start | bytes 6148
  64.7 53.9 %copy-start.1 = (bf16[1,16,1024]{2,1,0:T(8,128)(2,1)S(1)}, bf16[1,16,1024]{2,1,0:T(8,128)(2,1)}, u32[]{:S(2)}) copy-start(bf16[1,16,1024]{2,1,0:T(8,128)(2,1)} %param.6) | copy-start | bytes 98308
  67.9 51.1 %all-to-all-start.1 = ((bf16[128,8,1024]{2,1,0:T(8,128)(2,1)}), bf16[128,8,1024]{2,1,0:T(8,128)(2,1)}, u32[]{:S(2)}, u32[]{:S(2)}) async-start(bf16[128,8,1024]{2,1,0:T(8,128)(2,1)} %bitcast_select_fusion), calls=%async_computation.1 | async-start | bytes 4194304 | tf_op jit(solution)/shard_map/all_to_all | solution.py:48
  249.2 37.6 %all-to-all-start.2 = ((bf16[128,8,1024]{2,1,0:T(8,128)(2,1)}), bf16[128,8,1024]{2,1,0:T(8,128)(2,1)}, u32[]{:S(2)}, u32[]{:S(2)}) async-start(bf16[128,8,1024]{2,1,0:T(8,128)(2,1)} %scatter_fusion.1), calls=%async_computation.2 | async-start | bytes 4194304 | tf_op jit(solution)/shard_map/all_to_all | solution.py:86
  257.5 698.9 %reduce-scatter.4.cloned.1.call-start = ((), (), s32[]{:S(2)}) async-start(), calls=%async_computation.4 | async-start | bytes 4227072
  316.7 0.7 copy-start.3
Sparse Core Ops, SparseCore 0:
  316.8 639.5 reduce-scatter.3
where the time goes:
time: 968 us; the launch traced here: 964 us
  waiting for transfers between devices  583 us (60%)
  blocking collectives  158 us (16%)
  local copies, waits for them, and re-layouts  125 us (13%)
  matrix products  29.3 us (3%)
  starting transfers between devices  28.6 us (3%)
  other arithmetic  24 us (2%)
  between operations  16.1 us (2%)
    unnamed x2, waiting for transfers between devices  554 us
    scatter x1, local copies, waits for them, and re-layouts, shards(): outgoing = jnp.zeros((devices, capacity, model_width), jnp.bfloat16).at[o...  73 us
    unnamed x1, blocking collectives  72.1 us
    all_gather x1, blocking collectives, shards(): lax.all_gather(teacher_own, 'pair', axis=1, tiled=True)  41.4 us
    all_to_all x1, waiting for transfers between devices, shards(): lax.all_to_all(outgoing, ('group', 'pair'), split_axis=0, concat_axis=0,...  28.3 us
    all_gather x1, blocking collectives, shards(): grad_all = lax.all_gather(rank_grad, 'pair', axis=1, tiled=True)  22.6 us
    all_gather x1, blocking collectives, shards(): lax.all_gather(scores, 'pair', axis=1, tiled=True)  22 us
    scatter x1, local copies, waits for them, and re-layouts, shards(): jnp.zeros((devices, capacity), jnp.int32).at[owner_dev, slot_index]  22 us
  transfers between devices with their start and end apart: 4, of which 3 were waited for; matrix products, arithmetic and copies ran while one was open for 2% of the time, Pallas kernels for 0%

commit v1 on v0

--- a/solution.py
+++ b/solution.py
@@ -5,6 +5,33 @@
 from jax.sharding import PartitionSpec as P
 
 loss_scale = 1024.0
+
+
+def link_wall_all(here_x, axis_name):
+    z = lax.axis_size(axis_name)
+    d_next = lax.axis_index(axis_name)
+    small, kept_arr, upper = (z, d_next, here_x.shape[1])
+    slots = []
+    for j0 in range(small):
+        slots.append((j0, (j0 + 1) % small))
+    table = []
+    for j0 in range(small):
+        table.append((j0, (j0 - 1) % small))
+    long_array = jnp.zeros((*here_x.shape[:1], small * upper, *here_x.shape[2:]), here_x.dtype)
+    long_array = lax.dynamic_update_slice_in_dim(long_array, here_x, kept_arr * upper, axis=1)
+    moved = tmp = here_x
+    item_now = small // 2
+    for hop_no in range(1, item_now + 1):
+        moved = lax.ppermute(moved, axis_name, slots)
+        long_array = lax.dynamic_update_slice_in_dim(
+            long_array, moved, (kept_arr - hop_no) % small * upper, axis=1
+        )
+        if hop_no < small - item_now:
+            tmp = lax.ppermute(tmp, axis_name, table)
+            long_array = lax.dynamic_update_slice_in_dim(
+                long_array, tmp, (kept_arr + hop_no) % small * upper, axis=1
+            )
+    return long_array
 
 
 def soft_steps(values_all, values_own):
@@ -54,7 +81,7 @@
     teacher_own = teacher_scores.reshape(query_rows, cand_dev)
     scores_all, teacher_all = (
         lax.all_gather(scores, "pair", axis=1, tiled=True),
-        lax.all_gather(teacher_own, "pair", axis=1, tiled=True),
+        link_wall_all(teacher_own, "pair"),
     )
     soft_step = soft_steps(scores_all, scores)
     rank_student = 0.5 + jnp.sum(soft_step, -1)

time: 968 us -> 1000 us (1.033)
  blocking collectives: 158 us -> 117 us
  starting transfers between devices: 28.6 us -> 65 us
  waiting for transfers between devices: 583 us -> 618 us
    all_gather x1 -> x0, blocking collectives: 41.4 us -> none  [shards(): lax.all_gather(teacher_own, 'pair', axis=1, tiled=True)]
    ppermute x0 -> x15, starting transfers between devices: none -> 36.5 us  [the longest x7 36.4 us: link_wall_all(): tmp = lax.ppermute(tmp, axis_name, table)]
    ppermute x0 -> x15, waiting for transfers between devices: none -> 34.3 us  [the longest x8 34.3 us: link_wall_all(): moved = lax.ppermute(moved, axis_name, slots)]
  transfers between devices with their start and end apart: 4 -> 19, of which waited for: 3 -> 11; matrix products, arithmetic and copies ran while one was open for 2% -> 3% of each run, Pallas kernels for 0% -> 0%
where the time goes in v1:
time: 1000 us; the launch traced here: 998 us
  waiting for transfers between devices  618 us (62%)
  local copies, waits for them, and re-layouts  130 us (13%)
  blocking collectives  117 us (12%)
  starting transfers between devices  65 us (6%)
  matrix products  29.3 us (3%)
  other arithmetic  24 us (2%)
  between operations  16.1 us (2%)
    unnamed x2, waiting for transfers between devices  554 us
    scatter x1, local copies, waits for them, and re-layouts, shards(): outgoing = jnp.zeros((devices, capacity, model_width), jnp.bfloat16).at[o...  73 us
    unnamed x1, blocking collectives  72.1 us
    ppermute x7, starting transfers between devices, link_wall_all(): tmp = lax.ppermute(tmp, axis_name, table)  36.4 us
    ppermute x8, waiting for transfers between devices, link_wall_all(): moved = lax.ppermute(moved, axis_name, slots)  34.3 us
    all_to_all x1, waiting for transfers between devices, shards(): lax.all_to_all(outgoing, ('group', 'pair'), split_axis=0, concat_axis=0,...  28.1 us
    all_gather x1, blocking collectives, shards(): grad_all = lax.all_gather(rank_grad, 'pair', axis=1, tiled=True)  23.8 us
    scatter x1, local copies, waits for them, and re-layouts, shards(): jnp.zeros((devices, capacity), jnp.int32).at[owner_dev, slot_index]  22 us
  transfers between devices with their start and end apart: 19, of which 11 were waited for; matrix products, arithmetic and copies ran while one was open for 3% of the time, Pallas kernels for 0%

profile of v1, /device:TPU:0, one launch (start us, length us, event | category | flops | bytes accessed | tf_op | source)
XLA Modules:
  0.0 998.4 jit_solution(12052369414304187016)
XLA Ops:
  12.3 22.0 %scatter_fusion = s32[128,8]{0,1:T(8,128)S(1)} fusion(s32[128,8]{0,1:T(8,128)S(1)} %broadcast_in_dim.18, s32[512]{0:T(512)S(1)} %bitcast.81, s32[512]{0:T(512)S(1)} %reshape.320), kind=kCustom, calls=%fused_computation.2 | custom fusion | bytes 10240 | tf_op jit(solution)/shard_map/scatter | solution.py:69
  35.0 11.1 %all-to-all-start = ((s32[128,1,8]{2,1,0:T(1,128)}), s32[128,1,8]{2,1,0:T(1,128)S(1)}, u32[]{:S(2)}, u32[]{:S(2)}) async-start(s32[128,1,8]{2,1,0:T(1,128)} %copy.29), calls=%async_computation | async-start | bytes 131072 | tf_op jit(solution)/shard_map/all_to_all | solution.py:71
  46.2 8.3 convolution_convert_fusion.1
  56.0 8.8 gather_fusion
  67.9 9.1 all-to-all-start.1
  81.5 22.1 %collective-permute-done = f32[16,32]{1,0:T(8,128)S(1)} collective-permute-done((f32[16,32]{1,0:T(8,128)S(1)}, f32[16,32]{1,0:T(8,128)S(1)}, u32[]{:S(2)}, u32[]{:S(2)}) %collective-permute-start) | collective-permute-done | bytes 2080 | tf_op jit(solution)/shard_map/ppermute | solution.py:25
  103.5 5.3 collective-permute-start.3
  110.5 5.3 collective-permute-start.5
  117.5 5.3 collective-permute-start.7
  124.5 5.3 collective-permute-start.9
  131.4 5.3 collective-permute-start.11
  138.4 5.3 collective-permute-start.13
  152.9 7.7 gather_fusion.1
  161.0 20.9 %all-gather = f32[16,32,16]{1,2,0:T(8,128)S(1)} all-gather(f32[1,32,16]{1,2,0:T(8,128)S(1)} %get-tuple-element.28), channel_id=1, replica_groups=mesh['group'=8,'pair'=16] {'pair'}, dimensions={0}, use_global_device_ids=true | all-gather | bytes 34816 | tf_op jit(solution)/shard_map/all_gather | solution.py:83
  182.7 23.8 %all-gather.1 = f32[16,32,16]{1,2,0:T(8,128)S(1)} all-gather(f32[1,32,16]{1,2,0:T(8,128)S(1)} %multiply_bitcast_fusion), channel_id=1, replica_groups=mesh['group'=8,'pair'=16] {'pair'}, dimensions={0}, use_global_device_ids=true | all-gather | bytes 34816 | tf_op jit(solution)/shard_map/all_gather | solution.py:92
  210.2 73.0 %scatter_fusion.1 = bf16[128,8,1024]{2,1,0:T(8,128)(2,1)} fusion(bf16[128,8,1024]{2,1,0:T(8,128)(2,1)} %broadcast_in_dim.23, s32[512]{0:T(512)S(1)} %bitcast.82, bf16[512,1024]{1,0:T(8,128)(2,1)} %fusion.5), kind=kCustom, calls=%fused_computation.3 | custom fusion | bytes 3149824 | tf_op jit(solution)/shard_map/scatter | solution.py:111
  283.2 8.1 all-to-all-start.2
  292.4 28.1 %all-to-all-done.2 = bf16[128,8,1024]{2,1,0:T(8,128)(2,1)} async-done(((bf16[128,8,1024]{2,1,0:T(8,128)(2,1)}), bf16[128,8,1024]{2,1,0:T(8,128)(2,1)}, u32[]{:S(2)}, u32[]{:S(2)}) %all-to-all-start.2) | async-done | bytes 2097184 | tf_op jit(solution)/shard_map/all_to_all | solution.py:113
  320.5 13.4 %scatter_custom_fusion.2 = f32[2048,1024]{1,0:T(8,128)} fusion(s32[1024]{0:T(1024)S(1)} %bitcast.102, f32[]{:T(128)} %constant.174.clone.1, bf16[128,8,1024]{2,1,0:T(8,128)(2,1)} %all-to-all-done.2), kind=kCustom, calls=%fused_computation.5 | custom fusion | flops 2097152 | bytes 10485764 | tf_op jit(solution)/shard_map/scatter-add | solution.py:117
  333.9 11.2 %convolution_bitcast_fusion = f32[1024,1024]{0,1:T(8,128)} fusion(bf16[2048,1024]{1,0:T(8,128)(2,1)} %param.10, f32[2048,1024]{1,0:T(8,128)} %scatter_custom_fusion.2), kind=kOutput, calls=%fused_computation.10 | convolution fusion | flops 4297064448 | bytes 16777216 | tf_op jit(solution)/shard_map/pr,pe->re/dot_general | solution.py:124
  345.1 5.3 copy.37
  351.6 72.1 %all-reduce.2 = (bf16[16]{0:T(256)(128)(2,1)S(1)}, bf16[16,1024]{1,0:T(8,128)(2,1)S(1)}) all-reduce(bf16[16]{0:T(256)(128)(2,1)S(1)} %multiply_convert_fusion.1, bf16[16,1024]{1,0:T(8,128)(2,1)S(1)} %multiply_convert_fusion), channel_id=2, replica_groups=mesh['group'=8,'pair'=16] {'pair'}, use_global_device_ids=true, to_apply=%region_7.8.clone | all-reduce | flops 16400 | bytes 65600
  426.9 9.5 convolution_convert_fusion
  436.4 554.0 %reduce-scatter.4.cloned.1.call-done = f32[8,1024]{1,0:T(8,128)} async-done(((f32[1024,1024]{1,0:T(8,128)}), f32[8,1024]{1,0:T(8,128)}) %reduce-scatter.4.cloned.1.call-update) | async-done | bytes 32784
  (102 shorter events, 41.8 us)
Async XLA Ops:
  7.2 39.0 %copy-start = (bf16[1024,1024]{1,0:T(8,128)(2,1)S(1)}, bf16[1024,1024]{1,0:T(8,128)(2,1)}, u32[]{:S(2)}) copy-start(bf16[1024,1024]{1,0:T(8,128)(2,1)} %param.11) | copy-start | bytes 6291460
  35.0 20.6 %all-to-all-start = ((s32[128,1,8]{2,1,0:T(1,128)}), s32[128,1,8]{2,1,0:T(1,128)S(1)}, u32[]{:S(2)}, u32[]{:S(2)}) async-start(s32[128,1,8]{2,1,0:T(1,128)} %copy.29), calls=%async_computation | async-start | bytes 131072 | tf_op jit(solution)/shard_map/all_to_all | solution.py:71
  64.7 12.3 %copy-start.2 = (f32[1,1,16,32]{3,2,1,0:T(8,128)S(1)}, f32[1,1,16,32]{3,2,1,0:T(8,128)}, u32[]{:S(2)}) copy-start(f32[1,1,16,32]{3,2,1,0:T(8,128)} %param.7) | copy-start | bytes 6148
  64.7 16.7 %copy-start.1 = (bf16[1,16,1024]{2,1,0:T(8,128)(2,1)S(1)}, bf16[1,16,1024]{2,1,0:T(8,128)(2,1)}, u32[]{:S(2)}) copy-start(bf16[1,16,1024]{2,1,0:T(8,128)(2,1)} %param.6) | copy-start | bytes 98308
  67.9 85.0 %all-to-all-start.1 = ((bf16[128,8,1024]{2,1,0:T(8,128)(2,1)}), bf16[128,8,1024]{2,1,0:T(8,128)(2,1)}, u32[]{:S(2)}, u32[]{:S(2)}) async-start(bf16[128,8,1024]{2,1,0:T(8,128)(2,1)} %bitcast_select_fusion), calls=%async_computation.1 | async-start | bytes 4194304 | tf_op jit(solution)/shard_map/all_to_all | solution.py:75
  77.1 26.5 %collective-permute-start.1 = (f32[16,32]{1,0:T(8,128)S(1)}, f32[16,32]{1,0:T(8,128)S(1)}, u32[]{:S(2)}, u32[]{:S(2)}) collective-permute-start(f32[16,32]{1,0:T(8,128)S(1)} %bitcast.98), channel_id=1, source_target_pairs={{0,15},{1,0},{2,1},{3,2},{4,3},{5,4},{6,5},{7,6},{8,7},{9,8},{10,9... | collective-permute-start | bytes 6152 | tf_op jit(solution)/shard_map/ppermute | solution.py:30
  81.4 22.1 %collective-permute-start = (f32[16,32]{1,0:T(8,128)S(1)}, f32[16,32]{1,0:T(8,128)S(1)}, u32[]{:S(2)}, u32[]{:S(2)}) collective-permute-start(f32[16,32]{1,0:T(8,128)S(1)} %bitcast.99), channel_id=1, source_target_pairs={{0,1},{1,2},{2,3},{3,4},{4,5},{5,6},{6,7},{7,8},{8,9},{9,10},{10,1... | collective-permute-start | bytes 6152 | tf_op jit(solution)/shard_map/ppermute | solution.py:25
  103.5 7.0 collective-permute-start.2
  103.5 7.0 collective-permute-start.3
  110.5 7.0 collective-permute-start.4
  110.5 7.0 collective-permute-start.5
  117.5 7.0 collective-permute-start.6
  117.5 7.0 collective-permute-start.7
  124.5 7.0 collective-permute-start.8
  124.5 7.0 collective-permute-start.9
  131.4 7.0 collective-permute-start.10
  131.4 7.0 collective-permute-start.11
  138.4 7.0 collective-permute-start.12
  138.4 11.1 %collective-permute-start.13 = (f32[16,32]{1,0:T(8,128)S(1)}, f32[16,32]{1,0:T(8,128)S(1)}, u32[]{:S(2)}, u32[]{:S(2)}) collective-permute-start(f32[16,32]{1,0:T(8,128)S(1)} %collective-permute-done.11), channel_id=1, source_target_pairs={{0,15},{1,0},{2,1},{3,2},{4,3},{5,4},{6,5},{7,6},{8,7},{9,8},{10,9... | collective-permute-start | bytes 6152 | tf_op jit(solution)/shard_map/ppermute | solution.py:30
  145.4 7.0 collective-permute-start.14
  283.2 37.4 %all-to-all-start.2 = ((bf16[128,8,1024]{2,1,0:T(8,128)(2,1)}), bf16[128,8,1024]{2,1,0:T(8,128)(2,1)}, u32[]{:S(2)}, u32[]{:S(2)}) async-start(bf16[128,8,1024]{2,1,0:T(8,128)(2,1)} %scatter_fusion.1), calls=%async_computation.2 | async-start | bytes 4194304 | tf_op jit(solution)/shard_map/all_to_all | solution.py:113
  291.3 699.1 %reduce-scatter.4.cloned.1.call-start = ((), (), s32[]{:S(2)}) async-start(), calls=%async_computation.4 | async-start | bytes 4227072
  350.4 0.7 copy-start.3
Sparse Core Ops, SparseCore 0:
  350.6 639.7 reduce-scatter.3
